TPU v7x, 32 devices: a whole 2x2x4 slice. The times are simulated.
32 devices in a mesh: parts: 2 (over x), seq: 16 (over z, y, core).
Axes of the slice: x: 2, y: 2, z: 4, core: 2. Of those that a mesh axis runs over, the one named last changes fastest.
Arguments:
- tokens: bfloat16 [131072, 512], P(('parts', 'seq')), parts along dimension 0, may hold values from -6 to 6
- w_value: bfloat16 [512, 512], replicated, may hold values from -0.25 to 0.25
- w_gate: bfloat16 [512, 512], replicated, may hold values from -0.25 to 0.25
- first_block: bfloat16 [256, 256], replicated, may hold values from -0.375 to 0.375
- second_block: bfloat16 [256, 256], replicated, may hold values from -0.375 to 0.375
- third_block: bfloat16 [256, 256], replicated, may hold values from -0.375 to 0.375
- fourth_block: bfloat16 [256, 256], replicated, may hold values from -0.375 to 0.375
- kernel: bfloat16 [512, 256, 256], P('seq'), may hold values from -6 to 6
- skip_gain: float32 [512], replicated, may hold values from 0.25 to 2
- cotangent: bfloat16 [131072, 512], P(('parts', 'seq')), parts along dimension 0, may hold values from -6 to 6
Outputs:
- grad_tokens: bfloat16 [131072, 512], P(('parts', 'seq')), parts along dimension 0
- grad_kernel: bfloat16 [1024, 256, 256], P(('parts', 'seq')), parts along dimension 0
- grad_weights: float32 [4, 512, 512], P('parts'), parts along dimension 0
- grad_skip: float32 [1024], P('parts'), parts along dimension 0
There are 2 independent parts, one for each index of `parts`. A program takes and returns all parts, laid end to end along the dimension named above; an argument that names none is the same for every part. Nothing has to cross between parts.
All inputs are finite; a program needn't handle non-finite values.
Results may differ from a plain program's by a relative error of at most 0.025.
Values may be sent and summed in bfloat16 or wider, within the bound.
A program may use at most 128 MiB of HBM per device.

v0:
```python
import jax
import jax.numpy as jnp
from jax import lax
from jax.sharding import PartitionSpec as P

D = 512
N1 = 256
N2 = 256


def on_device(
    tokens,
    w_value,
    w_gate,
    first_block,
    second_block,
    third_block,
    fourth_block,
    kernel,
    skip_gain,
    cotangent,
):
    f32 = jnp.float32
    bf16 = jnp.bfloat16
    n_devices = lax.axis_size("seq")
    rows_here = N1 // n_devices
    local_rows = tokens.shape[0]
    value = jnp.dot(tokens, w_value, preferred_element_type=f32).astype(bf16)
    gate = jnp.dot(tokens, w_gate, preferred_element_type=f32).astype(bf16)
    cube = value.reshape(rows_here, N2, D)
    section_one = jnp.einsum("abc,pb->cap", cube, first_block, preferred_element_type=f32).astype(
        bf16
    )
    spectrum = jnp.einsum(
        "cap,qa->cqp",
        lax.all_to_all(section_one, "seq", split_axis=0, concat_axis=1, tiled=True),
        second_block,
        preferred_element_type=f32,
    )
    filtered = (spectrum * kernel.astype(f32)).astype(bf16)
    section_three = jnp.einsum(
        "cqp,rq->crp", filtered, third_block, preferred_element_type=f32
    ).astype(bf16)
    split_three = section_three.reshape(section_three.shape[0], n_devices, rows_here, N2)
    conv = jnp.einsum(
        "crp,sp->rsc",
        lax.all_to_all(split_three, "seq", split_axis=1, concat_axis=0, tiled=True)[:, 0],
        fourth_block,
        preferred_element_type=f32,
    )
    mixed = conv.reshape(local_rows, D) + skip_gain * value.astype(f32)
    upstream = cotangent.astype(f32)
    d_mix = (upstream * gate.astype(f32)).astype(bf16)
    d_gate = (upstream * mixed).astype(bf16)
    d_mix_cube = d_mix.reshape(rows_here, N2, D)
    d_three = jnp.einsum(
        "rsc,sp->crp", d_mix_cube, fourth_block, preferred_element_type=f32
    ).astype(bf16)
    d_freq = jnp.einsum(
        "crp,rq->cqp",
        lax.all_to_all(d_three, "seq", split_axis=0, concat_axis=1, tiled=True),
        third_block,
        preferred_element_type=f32,
    )
    grad_kernel = (d_freq * spectrum).astype(bf16)
    d_spec = (d_freq * kernel.astype(f32)).astype(bf16)
    d_one = jnp.einsum("cqp,qa->cap", d_spec, second_block, preferred_element_type=f32).astype(bf16)
    split_one = d_one.reshape(d_one.shape[0], n_devices, rows_here, N2)
    d_cube = jnp.einsum(
        "cap,pb->abc",
        lax.all_to_all(split_one, "seq", split_axis=1, concat_axis=0, tiled=True)[:, 0],
        first_block,
        preferred_element_type=f32,
    )
    d_value = (d_cube.reshape(local_rows, D) + skip_gain * d_mix.astype(f32)).astype(bf16)
    grad_tokens = (
        jnp.dot(d_value, w_value.T, preferred_element_type=f32)
        + jnp.dot(d_gate, w_gate.T, preferred_element_type=f32)
    ).astype(bf16)
    factor = 1.0 / jnp.sqrt(jnp.asarray(N1 * N2, f32))
    value_term = jnp.dot(tokens.T, d_value, preferred_element_type=f32) * factor
    gate_term = jnp.dot(tokens.T, d_gate, preferred_element_type=f32) * factor
    skip_term = jnp.sum(d_mix.astype(f32) * value.astype(f32), axis=0) * factor
    value_total, gate_total, skip_total = (
        lax.psum(value_term.astype(jnp.bfloat16), "seq").astype(jnp.float32),
        lax.psum(gate_term.astype(jnp.bfloat16), "seq").astype(jnp.float32),
        lax.psum(skip_term.astype(jnp.bfloat16), "seq").astype(jnp.float32),
    )
    return (grad_tokens, grad_kernel, jnp.stack([value_total, gate_total]), skip_total)


def solution(mesh):
    in_specs = (
        P(("parts", "seq"), None),
        P(),
        P(),
        P(),
        P(),
        P(),
        P(),
        P("seq", None, None),
        P(),
        P(("parts", "seq"), None),
    )
    out_specs = (
        P(("parts", "seq"), None),
        P(("parts", "seq"), None, None),
        P("parts", None, None),
        P("parts"),
    )
    return jax.shard_map(
        on_device, mesh=mesh, in_specs=in_specs, out_specs=out_specs, check_vma=False
    )
```

profile of v0, /device:TPU:0, one launch (start us, length us, event | category | flops | bytes accessed | tf_op | source)
XLA Modules:
  0.0 597.8 jit_solution(15915618487453710336)
XLA Ops:
  7.2 0.0 copy-start
  7.2 6.0 %fusion = bf16[4096,512]{1,0:T(8,128)(2,1)S(1)} fusion(bf16[4096,512]{1,0:T(8,128)(2,1)} %param.19, bf16[4096,512]{1,0:T(8,128)(2,1)} %param.10, bf16[512,512]{1,0:T(8,128)(2,1)} %param.12), kind=kOutput, calls=%fused_computation.7 | convolution fusion | flops 2157969408 | bytes 13107200 | tf_op jit(solution)/shard_map/dot_general | solution.py:29
  13.2 1.9 copy-done.5
  15.2 1.3 convert_bitcast_fusion.1
  16.5 4.4 copy.60
  20.9 7.5 %all-to-all-start = ((bf16[512,16,256]{2,1,0:T(8,128)(2,1)}), bf16[512,16,256]{2,1,0:T(8,128)(2,1)}, u32[]{:S(2)}, u32[]{:S(2)}) async-start(bf16[512,16,256]{2,1,0:T(8,128)(2,1)} %copy.60), calls=%async_computation | async-start | bytes 8388608 | tf_op jit(solution)/shard_map/all_to_all | solution.py:61
  28.4 0.0 copy-start.11
  28.4 4.6 convolution_convert_fusion
  33.0 0.0 copy-start.6
  33.0 2.0 copy-done.6
  35.0 1.3 convert_bitcast_fusion
  36.3 4.4 copy.70
  40.7 65.3 %all-to-all-done = bf16[512,16,256]{2,1,0:T(8,128)(2,1)} async-done(((bf16[512,16,256]{2,1,0:T(8,128)(2,1)}), bf16[512,16,256]{2,1,0:T(8,128)(2,1)}, u32[]{:S(2)}, u32[]{:S(2)}) %all-to-all-start) | async-done | bytes 4194336 | tf_op jit(solution)/shard_map/all_to_all | solution.py:61
  106.0 19.7 %all-to-all-start.2 = ((bf16[512,16,256]{2,1,0:T(8,128)(2,1)}), bf16[512,16,256]{2,1,0:T(8,128)(2,1)}, u32[]{:S(2)}, u32[]{:S(2)}) async-start(bf16[512,16,256]{2,1,0:T(8,128)(2,1)} %copy.70), calls=%async_computation.2 | async-start | bytes 8388608 | tf_op jit(solution)/shard_map/all_to_all | solution.py:36
  125.7 6.4 %copy.63 = bf16[32,256,256]{1,2,0:T(8,128)(2,1)} copy(bf16[32,256,256]{2,1,0:T(8,128)(2,1)} %param.17) | data formatting | bytes 8388608 | tf_op args[7]
  132.1 4.7 copy.61
  136.8 66.4 %all-to-all-done.2 = bf16[512,16,256]{2,1,0:T(8,128)(2,1)} async-done(((bf16[512,16,256]{2,1,0:T(8,128)(2,1)}), bf16[512,16,256]{2,1,0:T(8,128)(2,1)}, u32[]{:S(2)}, u32[]{:S(2)}) %all-to-all-start.2) | async-done | bytes 4194336 | tf_op jit(solution)/shard_map/all_to_all | solution.py:36
  203.2 2.8 copy.71
  206.0 0.6 copy-done.7
  206.7 1.3 fusion.30
  208.0 0.0 copy-start.2
  208.0 3.3 fusion.8
  211.3 2.2 copy-done.1
  213.6 1.3 fusion.16
  214.9 2.5 copy.74
  217.3 19.7 %all-to-all-start.3 = ((bf16[32,16,16,256]{3,2,0,1:T(8,128)(2,1)}), bf16[32,16,16,256]{3,2,0,1:T(8,128)(2,1)}, u32[]{:S(2)}, u32[]{:S(2)}) async-start(bf16[32,16,16,256]{3,2,0,1:T(8,128)(2,1)} %copy.74), calls=%async_computation.3 | async-start | bytes 8388608 | tf_op jit(solution)/shard_map/all_to_all | solution.py:47
  237.0 6.0 fusion.13
  243.0 2.3 copy.66
  245.4 69.2 %all-to-all-done.3 = bf16[32,16,16,256]{3,2,0,1:T(8,128)(2,1)} async-done(((bf16[32,16,16,256]{3,2,0,1:T(8,128)(2,1)}), bf16[32,16,16,256]{3,2,0,1:T(8,128)(2,1)}, u32[]{:S(2)}, u32[]{:S(2)}) %all-to-all-start.3) | async-done | bytes 4194336 | tf_op jit(solution)/shard_map/all_to_all | solution.py:47
  314.6 19.7 %all-to-all-start.1 = ((bf16[32,16,16,256]{3,2,0,1:T(8,128)(2,1)}), bf16[32,16,16,256]{3,2,0,1:T(8,128)(2,1)}, u32[]{:S(2)}, u32[]{:S(2)}) async-start(bf16[32,16,16,256]{3,2,0,1:T(8,128)(2,1)} %copy.66), calls=%async_computation.1 | async-start | bytes 8388608 | tf_op jit(solution)/shard_map/all_to_all | solution.py:71
  334.3 0.0 all-reduce.3.cloned.1.call-start
  334.3 6.4 %copy.76 = bf16[32,256,256]{2,1,0:T(8,128)(2,1)} copy(bf16[32,256,256]{1,2,0:T(8,128)(2,1)} %get-tuple-element.25) | data formatting | bytes 8388608
  340.7 3.7 copy.75
  344.4 4.5 fusion.32
  348.9 62.9 %all-to-all-done.1 = bf16[32,16,16,256]{3,2,0,1:T(8,128)(2,1)} async-done(((bf16[32,16,16,256]{3,2,0,1:T(8,128)(2,1)}), bf16[32,16,16,256]{3,2,0,1:T(8,128)(2,1)}, u32[]{:S(2)}, u32[]{:S(2)}) %all-to-all-start.1) | async-done | bytes 4194336 | tf_op jit(solution)/shard_map/all_to_all | solution.py:71
  411.8 3.8 copy.67
  415.7 4.5 fusion.24
  420.2 10.9 %fusion.7 = (f32[512]{0:T(512)S(1)}, bf16[4096,512]{1,0:T(8,128)(2,1)}, bf16[4096,512]{1,0:T(8,128)(2,1)S(1)}) fusion(bf16[4096,512]{1,0:T(8,128)(2,1)} %copy-done.6, bf16[4096,512]{1,0:T(8,128)(2,1)} %copy-done.5, f32[512]{0:T(512)S(1)} %copy-done.13, f32[512,16,256]{0,2,1:T(8,128)} %fusion.24, f32[512,16,256]{0,2,1:T(8,128)S(1)} %bitcast.101, ...), kind=kLoop, calls=%fused_computation.14 | loop fusion | flops 25165312 | bytes 37752832 | tf_op jit(solution)/shard_map/reduce_sum | solution.py:83
  431.0 8.2 %fusion.22 = bf16[1,512,512]{1,2,0:T(8,128)(2,1)} fusion(bf16[4096,512]{1,0:T(8,128)(2,1)} %get-tuple-element.23, bf16[4096,512]{1,0:T(8,128)(2,1)} %param.10), kind=kOutput, calls=%fused_computation.31 | convolution fusion | flops 2148007936 | bytes 8912896 | tf_op jit(solution)/shard_map/dot_general | solution.py:81
  439.2 5.9 fusion.35
  445.1 3.2 fusion.21
  448.3 47.8 %psum.23 = bf16[512]{0:T(512)(128)(2,1)S(1)} all-reduce(bf16[512]{0:T(512)(128)(2,1)S(1)} %multiply_convert_fusion), channel_id=1, replica_groups=mesh['parts'=2,'seq'=16] {'seq'}, use_global_device_ids=true, to_apply=%region_3.0 | all-reduce | flops 512 | bytes 2048 | tf_op jit(solution)/shard_map/psum | solution.py:87
  496.0 0.6 convert_element_type.116
  496.6 0.0 all-reduce.3.cloned.1.call-update
  496.6 9.2 %add_convert_fusion = bf16[4096,512]{1,0:T(8,128)(2,1)} fusion(f32[4096,512]{1,0:T(8,128)} %fusion.35, bf16[4096,512]{1,0:T(8,128)(2,1)} %copy-done.3, bf16[512,512]{1,0:T(8,128)(2,1)S(1)} %copy-done.12), kind=kOutput, calls=%fused_computation.17 | convolution fusion | flops 2151677952 | bytes 17301504 | tf_op jit(solution)/shard_map/dot_general | solution.py:78
  505.8 82.0 %all-reduce.3.cloned.1.call-done = (bf16[1,512,512]{1,2,0:T(8,128)(2,1)}, bf16[1,512,512]{1,2,0:T(8,128)(2,1)}) async-done(((bf16[1,512,512]{1,2,0:T(8,128)(2,1)}, bf16[1,512,512]{1,2,0:T(8,128)(2,1)}), (bf16[1,512,512]{1,2,0:T(8,128)(2,1)}, bf16[1,512,512]{1,2,0:T(8,128)(2,1)})) %all-reduce.3.cloned.1.call-update) | async-done | bytes 1048592 | tf_op jit(solution)/shard_map/psum | solution.py:86
  587.8 1.3 maximum_convert_fusion
  589.1 1.8 copy.77
  (28 shorter events, 0.1 us)
Async XLA Ops:
  7.2 21.3 %copy-start = (bf16[512,512]{1,0:T(8,128)(2,1)S(1)}, bf16[512,512]{1,0:T(8,128)(2,1)}, u32[]{:S(2)}) copy-start(bf16[512,512]{1,0:T(8,128)(2,1)} %param.11) | copy-start | bytes 1572868
  7.2 8.0 %copy-start.10 = (bf16[256,256]{1,0:T(8,128)(2,1)S(1)}, bf16[256,256]{1,0:T(8,128)(2,1)}, u32[]{:S(2)}) copy-start(bf16[256,256]{1,0:T(8,128)(2,1)} %param.16) | copy-start | bytes 393220
  13.2 1.9 copy-start.5
  20.9 85.0 %all-to-all-start = ((bf16[512,16,256]{2,1,0:T(8,128)(2,1)}), bf16[512,16,256]{2,1,0:T(8,128)(2,1)}, u32[]{:S(2)}, u32[]{:S(2)}) async-start(bf16[512,16,256]{2,1,0:T(8,128)(2,1)} %copy.60), calls=%async_computation | async-start | bytes 8388608 | tf_op jit(solution)/shard_map/all_to_all | solution.py:61
  28.4 6.6 %copy-start.11 = (bf16[256,256]{1,0:T(8,128)(2,1)S(1)}, bf16[256,256]{1,0:T(8,128)(2,1)}, u32[]{:S(2)}) copy-start(bf16[256,256]{1,0:T(8,128)(2,1)} %param.13) | copy-start | bytes 393220
  33.0 2.0 copy-start.6
  106.0 97.2 %all-to-all-start.2 = ((bf16[512,16,256]{2,1,0:T(8,128)(2,1)}), bf16[512,16,256]{2,1,0:T(8,128)(2,1)}, u32[]{:S(2)}, u32[]{:S(2)}) async-start(bf16[512,16,256]{2,1,0:T(8,128)(2,1)} %copy.70), calls=%async_computation.2 | async-start | bytes 8388608 | tf_op jit(solution)/shard_map/all_to_all | solution.py:36
  203.2 3.4 copy-start.7
  203.2 3.5 copy-start.8
  206.6 1.3 copy-start.9
  208.0 5.6 copy-start.1
  208.0 5.6 copy-start.2
  217.3 97.3 %all-to-all-start.3 = ((bf16[32,16,16,256]{3,2,0,1:T(8,128)(2,1)}), bf16[32,16,16,256]{3,2,0,1:T(8,128)(2,1)}, u32[]{:S(2)}, u32[]{:S(2)}) async-start(bf16[32,16,16,256]{3,2,0,1:T(8,128)(2,1)} %copy.74), calls=%async_computation.3 | async-start | bytes 8388608 | tf_op jit(solution)/shard_map/all_to_all | solution.py:47
  314.6 97.2 %all-to-all-start.1 = ((bf16[32,16,16,256]{3,2,0,1:T(8,128)(2,1)}), bf16[32,16,16,256]{3,2,0,1:T(8,128)(2,1)}, u32[]{:S(2)}, u32[]{:S(2)}) async-start(bf16[32,16,16,256]{3,2,0,1:T(8,128)(2,1)} %copy.66), calls=%async_computation.1 | async-start | bytes 8388608 | tf_op jit(solution)/shard_map/all_to_all | solution.py:71
  334.3 253.5 %all-reduce.3.cloned.1.call-start = ((), (), s32[]{:S(2)}) async-start(), calls=%async_computation.4 | async-start | bytes 2097152 | tf_op jit(solution)/shard_map/psum | solution.py:86
  411.8 8.3 %slice-start = ((s8[8388608]{0:T(1024)(128)(4,1)}), s8[4194304]{0:T(1024)(128)(4,1)S(1)}, s32[]{:S(2)}) async-start(s8[8388608]{0:T(1024)(128)(4,1)} %bitcast.100), calls=%async_computation.5 | async-start | bytes 8388608
  415.6 4.5 slice-start.1
  415.6 4.5 copy-start.13
  431.0 14.1 %copy-start.3 = (bf16[4096,512]{1,0:T(8,128)(2,1)}, bf16[4096,512]{1,0:T(8,128)(2,1)S(1)}, u32[]{:S(2)}) copy-start(bf16[4096,512]{1,0:T(8,128)(2,1)S(1)} %get-tuple-element.24) | copy-start | bytes 12582916
  431.0 8.2 %copy-start.4 = (bf16[4096,512]{1,0:T(8,128)(2,1)S(1)}, bf16[4096,512]{1,0:T(8,128)(2,1)}, u32[]{:S(2)}) copy-start(bf16[4096,512]{1,0:T(8,128)(2,1)} %get-tuple-element.23) | copy-start | bytes 12582916
  439.2 5.9 copy-start.14
  445.1 51.5 %copy-start.12 = (bf16[512,512]{1,0:T(8,128)(2,1)S(1)}, bf16[512,512]{1,0:T(8,128)(2,1)}, u32[]{:S(2)}) copy-start(bf16[512,512]{1,0:T(8,128)(2,1)} %param.12) | copy-start | bytes 1572868
Sparse Core Ops, SparseCore 0:
  496.8 90.9 all-reduce.2
where the time goes:
time: 599 us; the launch traced here: 598 us
  waiting for transfers between devices  346 us (58%)
  starting transfers between devices  66.6 us (11%)
  matrix products  60.6 us (10%)
  local copies, waits for them, and re-layouts  50.1 us (8%)
  blocking collectives  47.8 us (8%)
  between operations  14.3 us (2%)
  other arithmetic  12.8 us (2%)
    psum x1, waiting for transfers between devices, on_device(): lax.psum(gate_term.astype(jnp.bfloat16), 'seq').astype(jnp.float32)  82 us
    all_to_all x1, waiting for transfers between devices, on_device(): lax.all_to_all(split_three, 'seq', split_axis=1, concat_axis=0, tiled=True)  69.2 us
    all_to_all x1, waiting for transfers between devices, on_device(): lax.all_to_all(section_one, 'seq', split_axis=0, concat_axis=1, tiled=True)  66.4 us
    all_to_all x1, waiting for transfers between devices, on_device(): lax.all_to_all(d_three, 'seq', split_axis=0, concat_axis=1, tiled=True)  65.3 us
    all_to_all x1, waiting for transfers between devices, on_device(): lax.all_to_all(split_one, 'seq', split_axis=1, concat_axis=0, tiled=True)  62.9 us
    psum x1, blocking collectives, on_device(): lax.psum(skip_term.astype(jnp.bfloat16), 'seq').astype(jnp.float32)  47.8 us
    unnamed x37, local copies, waits for them, and re-layouts  21.5 us
    all_to_all x1, starting transfers between devices, on_device(): lax.all_to_all(split_three, 'seq', split_axis=1, concat_axis=0, tiled=True)  19.7 us
  transfers between devices with their start and end apart: 5, of which 5 were waited for; matrix products, arithmetic and copies ran while one was open for 9% of the time, Pallas kernels for 0%

commit v1 on v0

--- a/solution.py
+++ b/solution.py
@@ -83,7 +83,7 @@
     skip_term = jnp.sum(d_mix.astype(f32) * value.astype(f32), axis=0) * factor
     value_total, gate_total, skip_total = (
         lax.psum(value_term.astype(jnp.bfloat16), "seq").astype(jnp.float32),
-        lax.psum(gate_term.astype(jnp.bfloat16), "seq").astype(jnp.float32),
+        jnp.sum(lax.all_gather(gate_term.astype(jnp.bfloat16), "seq"), axis=0).astype(jnp.float32),
         lax.psum(skip_term.astype(jnp.bfloat16), "seq").astype(jnp.float32),
     )
     return (grad_tokens, grad_kernel, jnp.stack([value_total, gate_total]), skip_total)

time: 599 us -> 640 us (1.068)
  waiting for transfers between devices: 346 us -> 360 us
  local copies, waits for them, and re-layouts: 50.1 us -> 63.2 us
  other arithmetic: 12.8 us -> 21 us
    all_gather x0 -> x1, waiting for transfers between devices: none -> 16.5 us  [on_device(): lax.all_gather(gate_term.astype(jnp.bfloat16), 'seq')]
    unnamed x37 -> x38, local copies, waits for them, and re-layouts: 21.5 us -> 34.6 us
    psum x1, waiting for transfers between devices: 82 us -> 73 us  [on_device(): lax.psum(value_term.astype(jnp.bfloat16), 'seq').astype(jnp.float32)]
    reduce_sum x0 -> x1, other arithmetic: none -> 8.35 us  [on_device(): jnp.sum(lax.all_gather(gate_term.astype(jnp.bfloat16), 'seq'), axis=0)]
    all_to_all x1, waiting for transfers between devices: 62.9 us -> 69.3 us  [on_device(): lax.all_to_all(split_one, 'seq', split_axis=1, concat_axis=0, tiled=True)]
  transfers between devices with their start and end apart: 5 -> 6, of which waited for: 5 -> 6; matrix products, arithmetic and copies ran while one was open for 9% -> 13% of each run, Pallas kernels for 0% -> 0%
where the time goes in v1:
time: 640 us; the launch traced here: 635 us
  waiting for transfers between devices  360 us (56%)
  starting transfers between devices  67.3 us (11%)
  local copies, waits for them, and re-layouts  63.2 us (10%)
  matrix products  59.6 us (9%)
  blocking collectives  49.3 us (8%)
  other arithmetic  21 us (3%)
  between operations  14.5 us (2%)
    psum x1, waiting for transfers between devices, on_device(): lax.psum(value_term.astype(jnp.bfloat16), 'seq').astype(jnp.float32)  73 us
    all_to_all x1, waiting for transfers between devices, on_device(): lax.all_to_all(split_one, 'seq', split_axis=1, concat_axis=0, tiled=True)  69.3 us
    all_to_all x1, waiting for transfers between devices, on_device(): lax.all_to_all(split_three, 'seq', split_axis=1, concat_axis=0, tiled=True)  69.2 us
    all_to_all x1, waiting for transfers between devices, on_device(): lax.all_to_all(section_one, 'seq', split_axis=0, concat_axis=1, tiled=True)  66.4 us
    all_to_all x1, waiting for transfers between devices, on_device(): lax.all_to_all(d_three, 'seq', split_axis=0, concat_axis=1, tiled=True)  65.2 us
    psum x1, blocking collectives, on_device(): lax.psum(skip_term.astype(jnp.bfloat16), 'seq').astype(jnp.float32)  49.3 us
    unnamed x38, local copies, waits for them, and re-layouts  34.6 us
    all_to_all x1, starting transfers between devices, on_device(): lax.all_to_all(split_three, 'seq', split_axis=1, concat_axis=0, tiled=True)  19.9 us
  transfers between devices with their start and end apart: 6, of which 6 were waited for; matrix products, arithmetic and copies ran while one was open for 13% of the time, Pallas kernels for 0%

profile of v1, /device:TPU:0, one launch (start us, length us, event | category | flops | bytes accessed | tf_op | source)
XLA Modules:
  0.0 634.6 jit_solution(11578867936475679422)
XLA Ops:
  7.2 6.0 fusion
  13.2 2.0 copy-done.5
  15.3 1.3 convert_bitcast_fusion.1
  16.6 4.4 copy.60
  21.0 8.0 %all-to-all-start = ((bf16[512,16,256]{2,1,0:T(8,128)(2,1)}), bf16[512,16,256]{2,1,0:T(8,128)(2,1)}, u32[]{:S(2)}, u32[]{:S(2)}) async-start(bf16[512,16,256]{2,1,0:T(8,128)(2,1)} %copy.60), calls=%async_computation | async-start | bytes 8388608 | tf_op jit(solution)/shard_map/all_to_all | solution.py:61
  29.0 4.6 convolution_convert_fusion
  33.6 2.0 copy-done.6
  35.6 1.3 convert_bitcast_fusion
  36.9 4.4 copy.70
  41.3 65.2 %all-to-all-done = bf16[512,16,256]{2,1,0:T(8,128)(2,1)} async-done(((bf16[512,16,256]{2,1,0:T(8,128)(2,1)}), bf16[512,16,256]{2,1,0:T(8,128)(2,1)}, u32[]{:S(2)}, u32[]{:S(2)}) %all-to-all-start) | async-done | bytes 4194336 | tf_op jit(solution)/shard_map/all_to_all | solution.py:61
  106.5 19.7 %all-to-all-start.2 = ((bf16[512,16,256]{2,1,0:T(8,128)(2,1)}), bf16[512,16,256]{2,1,0:T(8,128)(2,1)}, u32[]{:S(2)}, u32[]{:S(2)}) async-start(bf16[512,16,256]{2,1,0:T(8,128)(2,1)} %copy.70), calls=%async_computation.2 | async-start | bytes 8388608 | tf_op jit(solution)/shard_map/all_to_all | solution.py:36
  126.2 6.4 %copy.63 = bf16[32,256,256]{1,2,0:T(8,128)(2,1)} copy(bf16[32,256,256]{2,1,0:T(8,128)(2,1)} %param.17) | data formatting | bytes 8388608 | tf_op args[7]
  132.6 4.7 copy.61
  137.3 66.4 %all-to-all-done.2 = bf16[512,16,256]{2,1,0:T(8,128)(2,1)} async-done(((bf16[512,16,256]{2,1,0:T(8,128)(2,1)}), bf16[512,16,256]{2,1,0:T(8,128)(2,1)}, u32[]{:S(2)}, u32[]{:S(2)}) %all-to-all-start.2) | async-done | bytes 4194336 | tf_op jit(solution)/shard_map/all_to_all | solution.py:36
  203.7 2.8 copy.71
  206.5 0.6 copy-done.7
  207.2 1.3 fusion.30
  208.5 3.3 fusion.8
  211.8 2.2 copy-done.1
  214.1 1.3 fusion.16
  215.4 2.5 copy.74
  217.9 19.9 %all-to-all-start.3 = ((bf16[32,16,16,256]{3,2,0,1:T(8,128)(2,1)}), bf16[32,16,16,256]{3,2,0,1:T(8,128)(2,1)}, u32[]{:S(2)}, u32[]{:S(2)}) async-start(bf16[32,16,16,256]{3,2,0,1:T(8,128)(2,1)} %copy.74), calls=%async_computation.3 | async-start | bytes 8388608 | tf_op jit(solution)/shard_map/all_to_all | solution.py:47
  237.7 6.0 fusion.13
  243.7 2.4 copy.66
  246.1 69.2 %all-to-all-done.3 = bf16[32,16,16,256]{3,2,0,1:T(8,128)(2,1)} async-done(((bf16[32,16,16,256]{3,2,0,1:T(8,128)(2,1)}), bf16[32,16,16,256]{3,2,0,1:T(8,128)(2,1)}, u32[]{:S(2)}, u32[]{:S(2)}) %all-to-all-start.3) | async-done | bytes 4194336 | tf_op jit(solution)/shard_map/all_to_all | solution.py:47
  315.3 19.7 %all-to-all-start.1 = ((bf16[32,16,16,256]{3,2,0,1:T(8,128)(2,1)}), bf16[32,16,16,256]{3,2,0,1:T(8,128)(2,1)}, u32[]{:S(2)}, u32[]{:S(2)}) async-start(bf16[32,16,16,256]{3,2,0,1:T(8,128)(2,1)} %copy.66), calls=%async_computation.1 | async-start | bytes 8388608 | tf_op jit(solution)/shard_map/all_to_all | solution.py:71
  335.0 0.0 all-gather.3.cloned.1.call-start
  335.0 3.7 copy.75
  338.7 4.5 fusion.32
  343.2 69.3 %all-to-all-done.1 = bf16[32,16,16,256]{3,2,0,1:T(8,128)(2,1)} async-done(((bf16[32,16,16,256]{3,2,0,1:T(8,128)(2,1)}), bf16[32,16,16,256]{3,2,0,1:T(8,128)(2,1)}, u32[]{:S(2)}, u32[]{:S(2)}) %all-to-all-start.1) | async-done | bytes 4194336 | tf_op jit(solution)/shard_map/all_to_all | solution.py:71
  412.5 3.8 copy.67
  416.3 4.5 fusion.24
  420.9 10.9 %fusion.7 = (f32[512]{0:T(512)S(1)}, bf16[4096,512]{1,0:T(8,128)(2,1)}, bf16[4096,512]{1,0:T(8,128)(2,1)S(1)}) fusion(bf16[4096,512]{1,0:T(8,128)(2,1)} %copy-done.6, bf16[4096,512]{1,0:T(8,128)(2,1)} %copy-done.5, f32[512]{0:T(512)S(1)} %copy-done.13, f32[512,16,256]{0,2,1:T(8,128)} %fusion.24, f32[512,16,256]{0,2,1:T(8,128)S(1)} %bitcast.105, ...), kind=kLoop, calls=%fused_computation.14 | loop fusion | flops 25165312 | bytes 37752832 | tf_op jit(solution)/shard_map/reduce_sum | solution.py:83
  431.7 2.0 copy-done.3
  433.7 5.3 fusion.21
  439.1 0.0 all-reduce.2.cloned.1.call-start
  439.2 6.4 %copy.76 = bf16[32,256,256]{2,1,0:T(8,128)(2,1)} copy(bf16[32,256,256]{1,2,0:T(8,128)(2,1)} %get-tuple-element.23) | data formatting | bytes 8388608
  445.6 49.3 %psum.15 = bf16[512]{0:T(512)(128)(2,1)S(1)} all-reduce(bf16[512]{0:T(512)(128)(2,1)S(1)} %multiply_convert_fusion), channel_id=1, replica_groups=mesh['parts'=2,'seq'=16] {'seq'}, use_global_device_ids=true, to_apply=%region_3.0 | all-reduce | flops 512 | bytes 2048 | tf_op jit(solution)/shard_map/psum | solution.py:87
  494.9 0.6 convert_element_type.129
  495.5 7.9 %fusion.35 = f32[4096,512]{1,0:T(8,128)} fusion(bf16[4096,512]{1,0:T(8,128)(2,1)} %get-tuple-element.21, bf16[512,512]{1,0:T(8,128)(2,1)S(1)} %copy-done), kind=kOutput, calls=%fused_computation.47 | convolution fusion | flops 2147483648 | bytes 13107200 | tf_op jit(solution)/shard_map/dot_general | solution.py:77
  503.4 3.2 fusion.22
  506.6 9.1 %add_convert_fusion = bf16[4096,512]{1,0:T(8,128)(2,1)} fusion(f32[4096,512]{1,0:T(8,128)} %fusion.35, bf16[4096,512]{1,0:T(8,128)(2,1)} %copy-done.3, bf16[512,512]{1,0:T(8,128)(2,1)S(1)} %copy-done.12), kind=kOutput, calls=%fused_computation.18 | convolution fusion | flops 2151677952 | bytes 17301504 | tf_op jit(solution)/shard_map/dot_general | solution.py:78
  515.7 16.5 %all-gather.3.cloned.1.call-done = bf16[8192,512]{0,1:T(8,128)(2,1)} async-done(((bf16[512,512]{0,1:T(8,128)(2,1)}), bf16[8192,512]{0,1:T(8,128)(2,1)}) %all-gather.3.cloned.1.call-update) | async-done | bytes 8388624 | tf_op jit(solution)/shard_map/all_gather | solution.py:86
  532.2 11.0 %copy.88 = bf16[64,8,16,512]{3,2,1,0:T(8,128)(2,1)} copy(bf16[64,8,16,512]{3,1,2,0:T(8,128)(2,1)} %bitcast.114) | data formatting | bytes 16777216
  543.2 8.4 %bitcast_reduce_fusion = bf16[512,512]{0,1:T(8,128)(2,1)S(1)} fusion(bf16[64,8,16,512]{3,2,1,0:T(8,128)(2,1)} %copy.88), kind=kLoop, calls=%fused_computation.15 | loop fusion | flops 3932160 | bytes 8912896 | tf_op jit(solution)/shard_map/reduce_sum | solution.py:86
  551.6 73.0 %all-reduce.2.cloned.1.call-done = bf16[1,512,512]{1,2,0:T(8,128)(2,1)} async-done(((bf16[1,512,512]{1,2,0:T(8,128)(2,1)}), bf16[1,512,512]{1,2,0:T(8,128)(2,1)}) %all-reduce.2.cloned.1.call-update) | async-done | bytes 524304 | tf_op jit(solution)/shard_map/psum | solution.py:85
  624.5 1.2 maximum_convert_fusion
  625.7 1.8 copy.77
  (33 shorter events, 0.1 us)
Async XLA Ops:
  7.2 21.8 %copy-start = (bf16[512,512]{1,0:T(8,128)(2,1)S(1)}, bf16[512,512]{1,0:T(8,128)(2,1)}, u32[]{:S(2)}) copy-start(bf16[512,512]{1,0:T(8,128)(2,1)} %param.11) | copy-start | bytes 1572868
  7.2 8.1 %copy-start.10 = (bf16[256,256]{1,0:T(8,128)(2,1)S(1)}, bf16[256,256]{1,0:T(8,128)(2,1)}, u32[]{:S(2)}) copy-start(bf16[256,256]{1,0:T(8,128)(2,1)} %param.16) | copy-start | bytes 393220
  13.2 2.0 copy-start.5
  21.0 85.5 %all-to-all-start = ((bf16[512,16,256]{2,1,0:T(8,128)(2,1)}), bf16[512,16,256]{2,1,0:T(8,128)(2,1)}, u32[]{:S(2)}, u32[]{:S(2)}) async-start(bf16[512,16,256]{2,1,0:T(8,128)(2,1)} %copy.60), calls=%async_computation | async-start | bytes 8388608 | tf_op jit(solution)/shard_map/all_to_all | solution.py:61
  29.0 6.6 %copy-start.11 = (bf16[256,256]{1,0:T(8,128)(2,1)S(1)}, bf16[256,256]{1,0:T(8,128)(2,1)}, u32[]{:S(2)}) copy-start(bf16[256,256]{1,0:T(8,128)(2,1)} %param.13) | copy-start | bytes 393220
  33.6 2.0 copy-start.6
  106.5 97.2 %all-to-all-start.2 = ((bf16[512,16,256]{2,1,0:T(8,128)(2,1)}), bf16[512,16,256]{2,1,0:T(8,128)(2,1)}, u32[]{:S(2)}, u32[]{:S(2)}) async-start(bf16[512,16,256]{2,1,0:T(8,128)(2,1)} %copy.70), calls=%async_computation.2 | async-start | bytes 8388608 | tf_op jit(solution)/shard_map/all_to_all | solution.py:36
  203.7 3.4 copy-start.7
  203.7 3.5 copy-start.8
  207.2 1.3 copy-start.9
  208.5 5.6 copy-start.1
  208.5 5.6 copy-start.2
  217.9 97.4 %all-to-all-start.3 = ((bf16[32,16,16,256]{3,2,0,1:T(8,128)(2,1)}), bf16[32,16,16,256]{3,2,0,1:T(8,128)(2,1)}, u32[]{:S(2)}, u32[]{:S(2)}) async-start(bf16[32,16,16,256]{3,2,0,1:T(8,128)(2,1)} %copy.74), calls=%async_computation.3 | async-start | bytes 8388608 | tf_op jit(solution)/shard_map/all_to_all | solution.py:47
  315.3 97.2 %all-to-all-start.1 = ((bf16[32,16,16,256]{3,2,0,1:T(8,128)(2,1)}), bf16[32,16,16,256]{3,2,0,1:T(8,128)(2,1)}, u32[]{:S(2)}, u32[]{:S(2)}) async-start(bf16[32,16,16,256]{3,2,0,1:T(8,128)(2,1)} %copy.66), calls=%async_computation.1 | async-start | bytes 8388608 | tf_op jit(solution)/shard_map/all_to_all | solution.py:71
  335.0 197.3 %all-gather.3.cloned.1.call-start = ((), (), s32[]{:S(2)}) async-start(), calls=%async_computation.5 | async-start | bytes 8912896 | tf_op jit(solution)/shard_map/all_gather | solution.py:86
  412.5 8.4 %slice-start = ((s8[8388608]{0:T(1024)(128)(4,1)}), s8[4194304]{0:T(1024)(128)(4,1)S(1)}, s32[]{:S(2)}) async-start(s8[8388608]{0:T(1024)(128)(4,1)} %bitcast.104), calls=%async_computation.6 | async-start | bytes 8388608
  416.3 4.6 slice-start.1
  416.3 4.5 copy-start.13
  431.7 2.0 copy-start.3
  439.1 185.4 %all-reduce.2.cloned.1.call-start = ((), (), s32[]{:S(2)}) async-start(), calls=%async_computation.4 | async-start | bytes 1048576 | tf_op jit(solution)/shard_map/psum | solution.py:85
  495.5 7.9 %copy-start.4 = (bf16[4096,512]{1,0:T(8,128)(2,1)S(1)}, bf16[4096,512]{1,0:T(8,128)(2,1)}, u32[]{:S(2)}) copy-start(bf16[4096,512]{1,0:T(8,128)(2,1)} %get-tuple-element.21) | copy-start | bytes 12582916
  495.5 7.9 %copy-start.14 = (bf16[4096,512]{1,0:T(8,128)(2,1)S(1)}, bf16[4096,512]{1,0:T(8,128)(2,1)}, u32[]{:S(2)}) copy-start(bf16[4096,512]{1,0:T(8,128)(2,1)} %param.10) | copy-start | bytes 12582916
  503.4 3.2 copy-start.12
Sparse Core Ops, SparseCore 0:
  439.2 92.9 all-gather.2
  535.6 88.8 all-reduce.1
